TPU v7x, 256 devices: a whole 4x4x8 slice. The times are simulated.
256 devices in a mesh: dp: 32 (over z, x_hi, core), tensor: 8 (over y, x_lo).
Axes of the slice: x: 4 (x_hi: 2, x_lo: 2; x = x_hi * 2 + x_lo), y: 4, z: 8, core: 2. Of those that a mesh axis runs over, the one named last changes fastest.
Arguments:
- grads: bfloat16 [32, 40, 128, 4096], P('dp', None, None, 'tensor'), may hold values from -6 to 6
- owner: int32 [40], replicated, may hold values from 0 to 31, as said below
- momentum: float32 [32, 2, 128, 4096], P('dp', None, None, 'tensor'), may hold values from -6 to 6, as said below
Outputs:
- update: bfloat16 [40, 128, 4096], P(None, None, 'tensor')
- new_momentum: float32 [32, 2, 128, 4096], P('dp', None, None, 'tensor')
Inputs may be any that keep to these rules, and one draw needn't show every extreme that they name: Every owner holds at least one matrix and no owner holds more than 2; some owner holds exactly 2. Slot s of owner p holds the momentum of the matrix of slot_rank s among those that owner p holds; slots beyond an owner's count hold values that are carried over.
All inputs are finite; a program needn't handle non-finite values.
Results may differ from a plain program's by a relative error of at most 0.03.
Values may be sent and summed in bfloat16 or wider, within the bound.
A program may use at most 64 MiB of HBM per device.

v0:
```python
import math
import jax
import jax.numpy as jnp
from jax import lax
from jax.sharding import PartitionSpec as P

R = 128
D = 4096
ITERS = 5
COEF_A = 3.4445
COEF_B = -4.775
COEF_C = 2.0315
EPSILON = 1e-07
DECAY = 0.95


def from_everyone(array, axis):
    copies = jnp.broadcast_to(array, (lax.axis_size(axis), *array.shape))
    return lax.all_to_all(copies, axis, split_axis=0, concat_axis=0, tiled=True)


def joined_along(pieces, dim):
    pieces = jnp.moveaxis(pieces, 0, dim)
    shape = pieces.shape
    return pieces.reshape(*shape[:dim], shape[dim] * shape[dim + 1], *shape[dim + 2 :])


def gathered_copies(array, axis, dim):
    pieces = from_everyone(array, axis)
    return joined_along(pieces, dim)


def next_polynomial(gram):
    gram = lax.optimization_barrier(gram)
    square = jnp.einsum("srt,stu->sru", gram, gram, preferred_element_type=jnp.float32)
    return (COEF_B * gram.astype(jnp.float32) + COEF_C * square).astype(jnp.bfloat16)


def apply_polynomial(polynomial, iterate):
    return COEF_A * iterate.astype(jnp.float32) + jnp.einsum(
        "srt,std->srd", polynomial, iterate, preferred_element_type=jnp.float32
    )


def orthogonalize_gathered(rounded, local_cols, factor):
    gathered = gathered_copies(rounded, "tensor", 2)
    squares = jnp.sum(jnp.square(gathered.astype(jnp.float32)), axis=(1, 2))
    iterate = (gathered.astype(jnp.float32) / (jnp.sqrt(squares)[:, None, None] + EPSILON)).astype(
        jnp.bfloat16
    )
    start = lax.axis_index("tensor") * local_cols
    following = None
    for step in range(ITERS):
        gram = jnp.einsum(
            "srd,std->srt", iterate, iterate, preferred_element_type=jnp.float32
        ).astype(jnp.bfloat16)
        polynomial = next_polynomial(gram)
        if step + 1 < ITERS:
            iterate = apply_polynomial(polynomial, iterate).astype(jnp.bfloat16)
        else:
            own_cols = lax.dynamic_slice_in_dim(iterate, start, local_cols, 2)
            following = apply_polynomial(polynomial, own_cols)
    return (factor * following).astype(jnp.bfloat16)


def per_device(grads, owner, momentum):
    owner_count = lax.axis_size("dp")
    myself = lax.axis_index("dp")
    matrices = owner.shape[0]
    slot_count = momentum.shape[1]
    head_rows = grads.shape[2]
    local_cols = grads.shape[3]
    piece_len = head_rows * local_cols // owner_count
    factor = 0.2 * math.sqrt(max(R, D))
    positions = jnp.arange(matrices, dtype=jnp.int32)
    same_owner = owner[:, None] == owner[None, :]
    earlier = positions[None, :] < positions[:, None]
    slot_rank = jnp.sum((same_owner & earlier).astype(jnp.int32), axis=1)
    owner_ids = jnp.arange(owner_count, dtype=jnp.int32)
    slot_ids = jnp.arange(slot_count, dtype=jnp.int32)
    matches = (owner[None, None, :] == owner_ids[:, None, None]) & (
        slot_rank[None, None, :] == slot_ids[None, :, None]
    )
    filled = jnp.any(matches, axis=2)
    source = jnp.sum(jnp.where(matches, positions[None, None, :], 0), axis=2)
    gradient = grads[0]
    zero_float = jnp.zeros((), jnp.float32)
    flattened = gradient.reshape(matrices, head_rows * local_cols).astype(jnp.float32)
    column_part = lax.psum_scatter(
        flattened.astype(jnp.bfloat16), "dp", scatter_dimension=1, tiled=True
    ).astype(jnp.float32)
    outgoing = jnp.take(column_part, source.T.reshape(-1), axis=0).reshape(
        slot_count, owner_count, piece_len
    )
    outgoing = jnp.where(filled.T[:, :, None], outgoing, zero_float)
    incoming = lax.all_to_all(outgoing, "dp", split_axis=1, concat_axis=1, tiled=True)
    mean_grad = incoming.reshape(slot_count, head_rows, local_cols) / owner_count
    previous = momentum[0]
    following = DECAY * previous + mean_grad
    held_here = lax.dynamic_index_in_dim(filled, myself, 0, keepdims=False)
    new_momentum = jnp.where(held_here[:, None, None], following, previous)[None]
    rounded = (mean_grad + DECAY * following).astype(jnp.bfloat16)
    result = orthogonalize_gathered(rounded, local_cols, factor)
    pieces = result.reshape(slot_count, owner_count, piece_len)
    returned = lax.all_to_all(pieces, "dp", split_axis=1, concat_axis=1, tiled=True)
    chosen = jnp.take(
        returned.reshape(slot_count * owner_count, piece_len),
        slot_rank * owner_count + owner,
        axis=0,
    )
    complete = lax.all_gather(chosen, "dp", axis=1, tiled=True)
    update = complete.reshape(matrices, head_rows, local_cols)
    return (update, new_momentum)


def solution(mesh):
    in_specs = (P("dp", None, None, "tensor"), P(), P("dp", None, None, "tensor"))
    out_specs = (P(None, None, "tensor"), P("dp", None, None, "tensor"))
    return jax.shard_map(
        per_device, mesh=mesh, in_specs=in_specs, out_specs=out_specs, check_vma=False
    )
```

profile of v0, /device:TPU:1, one launch (start us, length us, event | category | flops | bytes accessed | tf_op | source)
XLA Modules:
  0.0 357.7 jit_solution(3172155386606064688)
XLA Ops:
  7.2 0.0 reduce-scatter.2.cloned.1.call-start
  7.2 7.9 %copy.34 = bf16[5,8,128,512]{3,1,2,0:T(8,128)(2,1)} copy(bf16[5,8,128,512]{3,2,1,0:T(8,128)(2,1)} %bitcast.51) | data formatting | bytes 10485760
  15.1 0.0 reduce-scatter.2.cloned.1.call-update
  15.2 0.6 copy-done.4
  15.8 0.2 convert_reduce_fusion
  16.0 0.1 fusion.42
  16.1 0.1 reshape.137
  16.2 0.1 copy.27
  16.3 0.1 and_reduce_fusion
  16.4 0.1 copy.26
  16.5 131.4 %reduce-scatter.2.cloned.1.call-done = bf16[40,2048]{1,0:T(8,128)(2,1)} async-done(((bf16[40,65536]{1,0:T(8,128)(2,1)}), bf16[40,2048]{1,0:T(8,128)(2,1)}) %reduce-scatter.2.cloned.1.call-update) | async-done | bytes 163856 | tf_op jit(solution)/shard_map/reduce_scatter | solution.py:89
  147.9 0.9 convert_element_type.104
  148.9 0.8 gather_fusion
  149.7 0.6 fusion.20
  150.3 27.4 %all_to_all.15 = f32[2,32,2048]{2,0,1:T(2,128)S(1)} all-to-all(f32[2,32,2048]{2,0,1:T(2,128)S(1)} %fusion.20), channel_id=1, replica_groups=mesh['dp'=32,'tensor'=8] {'dp'}, dimensions={1} | all-to-all | bytes 1048576 | tf_op jit(solution)/shard_map/all_to_all | solution.py:96
  177.7 0.3 copy_multiply_fusion
  178.0 0.1 div.20
  178.2 0.1 fusion.19
  178.3 1.5 broadcast_in_dim.79
  179.8 4.9 %all-to-all-start.1 = ((bf16[8,2,128,512]{3,2,1,0:T(8,128)(2,1)}), bf16[8,2,128,512]{3,2,1,0:T(8,128)(2,1)S(1)}, u32[]{:S(2)}, u32[]{:S(2)}) async-start(bf16[8,2,128,512]{3,2,1,0:T(8,128)(2,1)} %broadcast_in_dim.79), calls=%async_computation.2 | async-start | bytes 4194304 | tf_op jit(solution)/shard_map/all_to_all | solution.py:19
  184.8 25.7 %all-to-all-done.1 = bf16[8,2,128,512]{3,2,1,0:T(8,128)(2,1)S(1)} async-done(((bf16[8,2,128,512]{3,2,1,0:T(8,128)(2,1)}), bf16[8,2,128,512]{3,2,1,0:T(8,128)(2,1)S(1)}, u32[]{:S(2)}, u32[]{:S(2)}) %all-to-all-start.1) | async-done | bytes 2097184 | tf_op jit(solution)/shard_map/all_to_all | solution.py:19
  210.4 0.7 fusion.4
  211.1 0.6 convert_bitcast_fusion
  211.7 0.6 copy.33
  212.3 0.4 divide_convert_fusion
  212.7 0.7 convolution_convert_fusion.4
  213.4 2.2 fusion
  215.7 3.1 convolution_convert_fusion.3
  218.8 2.2 fusion.1
  221.0 3.1 convolution_convert_fusion.2
  224.1 2.2 fusion.2
  226.3 3.1 convolution_convert_fusion.1
  229.4 2.2 fusion.3
  231.6 2.9 convolution_convert_fusion
  234.6 1.4 fusion.6
  236.0 0.2 reshape.138
  236.2 1.0 copy.31
  237.2 7.8 %all-to-all-start.2 = ((bf16[2,32,2048]{2,0,1:T(2,128)(2,1)}), bf16[2,32,2048]{2,0,1:T(2,128)(2,1)S(1)}, u32[]{:S(2)}, u32[]{:S(2)}) async-start(bf16[2,32,2048]{2,0,1:T(2,128)(2,1)} %copy.31), calls=%async_computation.3 | async-start | bytes 524288 | tf_op jit(solution)/shard_map/all_to_all | solution.py:105
  245.0 0.0 all-gather.2.cloned.1.call-start
  245.1 12.9 %all-to-all-done.2 = bf16[2,32,2048]{2,0,1:T(2,128)(2,1)S(1)} async-done(((bf16[2,32,2048]{2,0,1:T(2,128)(2,1)}), bf16[2,32,2048]{2,0,1:T(2,128)(2,1)S(1)}, u32[]{:S(2)}, u32[]{:S(2)}) %all-to-all-start.2) | async-done | bytes 262176 | tf_op jit(solution)/shard_map/all_to_all | solution.py:105
  257.9 0.1 copy.32
  258.0 0.7 gather_fusion.1
  258.7 0.8 broadcast_select_fusion
  259.5 0.2 dynamic-slice_reduce_fusion
  259.7 0.1 div.23
  259.8 1.0 add_select_fusion
  260.8 83.2 %all-gather.2.cloned.1.call-done = bf16[40,65536]{1,0:T(8,128)(2,1)} async-done(((bf16[40,2048]{1,0:T(8,128)(2,1)}), bf16[40,65536]{1,0:T(8,128)(2,1)}) %all-gather.2.cloned.1.call-update) | async-done | bytes 5242896 | tf_op jit(solution)/shard_map/all_gather | solution.py:111
  344.0 6.8 %copy.35 = bf16[5,8,128,512]{3,2,1,0:T(8,128)(2,1)} copy(bf16[5,8,128,512]{3,1,2,0:T(8,128)(2,1)} %bitcast.52) | data formatting | bytes 10485760
  (18 shorter events, 0.1 us)
Async XLA Ops:
  7.2 140.8 %reduce-scatter.2.cloned.1.call-start = ((), (), s32[]{:S(2)}) async-start(), calls=%async_computation.4 | async-start | bytes 5406720 | tf_op jit(solution)/shard_map/reduce_scatter | solution.py:89
  15.1 0.7 copy-start.4
  149.6 28.5 %copy-start.3 = (f32[1,2,128,512]{3,2,1,0:T(8,128)S(1)}, f32[1,2,128,512]{3,2,1,0:T(8,128)}, u32[]{:S(2)}) copy-start(f32[1,2,128,512]{3,2,1,0:T(8,128)} %param.5) | copy-start | bytes 1572868
  179.8 30.6 %all-to-all-start.1 = ((bf16[8,2,128,512]{3,2,1,0:T(8,128)(2,1)}), bf16[8,2,128,512]{3,2,1,0:T(8,128)(2,1)S(1)}, u32[]{:S(2)}, u32[]{:S(2)}) async-start(bf16[8,2,128,512]{3,2,1,0:T(8,128)(2,1)} %broadcast_in_dim.79), calls=%async_computation.2 | async-start | bytes 4194304 | tf_op jit(solution)/shard_map/all_to_all | solution.py:19
  215.7 3.1 copy-start
  221.0 3.1 copy-start.1
  226.3 3.1 copy-start.2
  237.2 20.8 %all-to-all-start.2 = ((bf16[2,32,2048]{2,0,1:T(2,128)(2,1)}), bf16[2,32,2048]{2,0,1:T(2,128)(2,1)S(1)}, u32[]{:S(2)}, u32[]{:S(2)}) async-start(bf16[2,32,2048]{2,0,1:T(2,128)(2,1)} %copy.31), calls=%async_computation.3 | async-start | bytes 524288 | tf_op jit(solution)/shard_map/all_to_all | solution.py:105
  245.0 99.0 %all-gather.2.cloned.1.call-start = ((), (), s32[]{:S(2)}) async-start(), calls=%async_computation.5 | async-start | bytes 5406720 | tf_op jit(solution)/shard_map/all_gather | solution.py:111
Sparse Core Ops, SparseCore 0:
  15.3 132.6 reduce-scatter.1
  259.6 84.3 all-gather.1
where the time goes:
time: 358 us
  waiting for transfers between devices  253 us (71%)
  blocking collectives  27.4 us (8%)
  matrix products  23.2 us (6%)
  local copies, waits for them, and re-layouts  21 us (6%)
  between operations  14.2 us (4%)
  starting transfers between devices  12.9 us (4%)
  other arithmetic  5.8 us (2%)
    reduce_scatter x1, waiting for transfers between devices, per_device(): lax.psum_scatter(flattened.astype(jnp.bfloat16), 'dp', scatter_dimension=...  131 us
    all_gather x1, waiting for transfers between devices, per_device(): complete = lax.all_gather(chosen, 'dp', axis=1, tiled=True)  83.2 us
    all_to_all x1, blocking collectives, per_device(): lax.all_to_all(outgoing, 'dp', split_axis=1, concat_axis=1, tiled=True)  27.4 us
    all_to_all x1, waiting for transfers between devices, from_everyone(): return lax.all_to_all(copies, axis, split_axis=0, concat_axis=0, tiled=True)  25.7 us
    unnamed x12, local copies, waits for them, and re-layouts  15.4 us
    dot_general x5, matrix products, orthogonalize_gathered(): jnp.einsum('srd,std->srt', iterate, iterate, preferred_element_type=jnp.f...  12.9 us
    all_to_all x1, waiting for transfers between devices, per_device(): lax.all_to_all(pieces, 'dp', split_axis=1, concat_axis=1, tiled=True)  12.9 us
    dot_general x5, matrix products, apply_polynomial(): jnp.einsum('srt,std->srd', polynomial, iterate, preferred_element_type=jn...  10.4 us
  transfers between devices with their start and end apart: 4, of which 4 were waited for; matrix products, arithmetic and copies ran while one was open for 1% of the time, Pallas kernels for 0%

commit v1 on v0

--- a/solution.py
+++ b/solution.py
@@ -108,7 +108,8 @@
         slot_rank * owner_count + owner,
         axis=0,
     )
-    complete = lax.all_gather(chosen, "dp", axis=1, tiled=True)
+    outgoing_2 = jnp.stack([chosen] * lax.axis_size("dp"))
+    complete = jnp.concatenate(lax.all_to_all(outgoing_2, "dp", 0, 0), axis=1)
     update = complete.reshape(matrices, head_rows, local_cols)
     return (update, new_momentum)
 

time: 358 us -> 409 us (1.14)
  waiting for transfers between devices: 253 us -> 285 us
  local copies, waits for them, and re-layouts: 21 us -> 34 us
  starting transfers between devices: 12.9 us -> 17.7 us
    all_to_all x0 -> x1, waiting for transfers between devices: none -> 115 us  [per_device(): complete = jnp.concatenate(lax.all_to_all(outgoing_2, 'dp', 0, 0), axis=1)]
    all_gather x1 -> x0, waiting for transfers between devices: 83.2 us -> none  [per_device(): complete = lax.all_gather(chosen, 'dp', axis=1, tiled=True)]
    another operation x0 -> x2, local copies, waits for them, and re-layouts: none -> 12.1 us  [the longest x1 9.1 us: per_device(): update = complete.reshape(matrices, head_rows, local_cols)]
    reshape x0 -> x1, local copies, waits for them, and re-layouts: none -> 7.7 us  [per_device(): complete = jnp.concatenate(lax.all_to_all(outgoing_2, 'dp', 0, 0), axis=1)]
    unnamed x12 -> x11, local copies, waits for them, and re-layouts: 15.4 us -> 8.56 us
    all_to_all x0 -> x1, starting transfers between devices: none -> 4.88 us  [per_device(): complete = jnp.concatenate(lax.all_to_all(outgoing_2, 'dp', 0, 0), axis=1)]
where the time goes in v1:
time: 409 us; the launch traced here: 407 us
  waiting for transfers between devices  285 us (70%)
  local copies, waits for them, and re-layouts  34 us (8%)
  blocking collectives  27.4 us (7%)
  matrix products  23.1 us (6%)
  starting transfers between devices  17.7 us (4%)
  between operations  14.2 us (3%)
  other arithmetic  5.13 us (1%)
    reduce_scatter x1, waiting for transfers between devices, per_device(): lax.psum_scatter(flattened.astype(jnp.bfloat16), 'dp', scatter_dimension=...  131 us
    all_to_all x1, waiting for transfers between devices, per_device(): complete = jnp.concatenate(lax.all_to_all(outgoing_2, 'dp', 0, 0), axis=1)  115 us
    all_to_all x1, blocking collectives, per_device(): lax.all_to_all(outgoing, 'dp', split_axis=1, concat_axis=1, tiled=True)  27.4 us
    all_to_all x1, waiting for transfers between devices, from_everyone(): return lax.all_to_all(copies, axis, split_axis=0, concat_axis=0, tiled=True)  25.7 us
    all_to_all x1, waiting for transfers between devices, per_device(): lax.all_to_all(pieces, 'dp', split_axis=1, concat_axis=1, tiled=True)  12.9 us
    dot_general x5, matrix products, orthogonalize_gathered(): jnp.einsum('srd,std->srt', iterate, iterate, preferred_element_type=jnp.f...  12.9 us
    dot_general x5, matrix products, apply_polynomial(): jnp.einsum('srt,std->srd', polynomial, iterate, preferred_element_type=jn...  10.3 us
    another operation x1, local copies, waits for them, and re-layouts, per_device(): update = complete.reshape(matrices, head_rows, local_cols)  9.1 us
  transfers between devices with their start and end apart: 4, of which 4 were waited for; matrix products, arithmetic and copies ran while one was open for 1% of the time, Pallas kernels for 0%

profile of v1, /device:TPU:1, one launch (start us, length us, event | category | flops | bytes accessed | tf_op | source)
XLA Modules:
  0.0 406.7 jit_solution(10990777191001387982)
XLA Ops:
  7.2 7.9 %copy.37 = bf16[5,8,128,512]{3,1,2,0:T(8,128)(2,1)} copy(bf16[5,8,128,512]{3,2,1,0:T(8,128)(2,1)} %bitcast.50) | data formatting | bytes 10485760
  15.2 0.6 copy-done.4
  15.8 0.2 convert_reduce_fusion
  16.0 0.1 fusion.42
  16.1 0.1 reshape.145
  16.2 0.1 copy.29
  16.3 0.1 and_reduce_fusion
  16.4 0.1 copy.28
  16.5 131.4 %reduce-scatter.2.cloned.1.call-done = bf16[40,2048]{1,0:T(8,128)(2,1)} async-done(((bf16[40,65536]{1,0:T(8,128)(2,1)}), bf16[40,2048]{1,0:T(8,128)(2,1)}) %reduce-scatter.2.cloned.1.call-update) | async-done | bytes 163856 | tf_op jit(solution)/shard_map/reduce_scatter | solution.py:89
  147.9 0.9 convert_element_type.104
  148.9 0.8 gather_fusion
  149.7 0.6 fusion.20
  150.3 27.4 %all_to_all.20 = f32[2,32,2048]{2,0,1:T(2,128)S(1)} all-to-all(f32[2,32,2048]{2,0,1:T(2,128)S(1)} %fusion.20), channel_id=1, replica_groups=mesh['dp'=32,'tensor'=8] {'dp'}, dimensions={1} | all-to-all | bytes 1048576 | tf_op jit(solution)/shard_map/all_to_all | solution.py:96
  177.7 0.3 copy_multiply_fusion
  178.0 0.1 div.20
  178.2 0.1 fusion.19
  178.3 1.5 broadcast_in_dim.79
  179.8 4.9 %all-to-all-start.1 = ((bf16[8,2,128,512]{3,2,1,0:T(8,128)(2,1)}), bf16[8,2,128,512]{3,2,1,0:T(8,128)(2,1)S(1)}, u32[]{:S(2)}, u32[]{:S(2)}) async-start(bf16[8,2,128,512]{3,2,1,0:T(8,128)(2,1)} %broadcast_in_dim.79), calls=%async_computation.2 | async-start | bytes 4194304 | tf_op jit(solution)/shard_map/all_to_all | solution.py:19
  184.8 25.7 %all-to-all-done.1 = bf16[8,2,128,512]{3,2,1,0:T(8,128)(2,1)S(1)} async-done(((bf16[8,2,128,512]{3,2,1,0:T(8,128)(2,1)}), bf16[8,2,128,512]{3,2,1,0:T(8,128)(2,1)S(1)}, u32[]{:S(2)}, u32[]{:S(2)}) %all-to-all-start.1) | async-done | bytes 2097184 | tf_op jit(solution)/shard_map/all_to_all | solution.py:19
  210.4 0.7 fusion.4
  211.1 0.6 convert_bitcast_fusion
  211.7 0.6 copy.36
  212.3 0.4 divide_convert_fusion
  212.7 0.7 convolution_convert_fusion.4
  213.4 2.2 fusion
  215.7 3.1 convolution_convert_fusion.3
  218.8 2.2 fusion.1
  221.0 3.1 convolution_convert_fusion.2
  224.1 2.2 fusion.2
  226.3 3.1 convolution_convert_fusion.1
  229.4 2.2 fusion.3
  231.6 2.9 convolution_convert_fusion
  234.6 1.4 fusion.6
  235.9 0.2 reshape.146
  236.1 1.0 copy.33
  237.1 7.9 %all-to-all-start.2 = ((bf16[2,32,2048]{2,0,1:T(2,128)(2,1)}), bf16[2,32,2048]{2,0,1:T(2,128)(2,1)S(1)}, u32[]{:S(2)}, u32[]{:S(2)}) async-start(bf16[2,32,2048]{2,0,1:T(2,128)(2,1)} %copy.33), calls=%async_computation.3 | async-start | bytes 524288 | tf_op jit(solution)/shard_map/all_to_all | solution.py:105
  245.0 12.9 %all-to-all-done.2 = bf16[2,32,2048]{2,0,1:T(2,128)(2,1)S(1)} async-done(((bf16[2,32,2048]{2,0,1:T(2,128)(2,1)}), bf16[2,32,2048]{2,0,1:T(2,128)(2,1)S(1)}, u32[]{:S(2)}, u32[]{:S(2)}) %all-to-all-start.2) | async-done | bytes 262176 | tf_op jit(solution)/shard_map/all_to_all | solution.py:105
  257.9 0.1 copy.34
  258.0 0.7 gather_fusion.1
  258.6 0.1 broadcast_select_fusion
  258.7 3.0 stack.2
  261.8 4.9 %all-to-all-start.3 = ((bf16[32,40,2048]{2,1,0:T(8,128)(2,1)}), bf16[32,40,2048]{2,1,0:T(8,128)(2,1)}, u32[]{:S(2)}, u32[]{:S(2)}) async-start(bf16[32,40,2048]{2,1,0:T(8,128)(2,1)} %stack.2), calls=%async_computation.4 | async-start | bytes 10485760 | tf_op jit(solution)/shard_map/all_to_all | solution.py:112
  266.6 0.2 dynamic-slice_reduce_fusion
  266.8 0.1 div.23
  267.0 1.0 add_select_fusion
  267.9 115.1 %all-to-all-done.3 = bf16[32,40,2048]{2,1,0:T(8,128)(2,1)} async-done(((bf16[32,40,2048]{2,1,0:T(8,128)(2,1)}), bf16[32,40,2048]{2,1,0:T(8,128)(2,1)}, u32[]{:S(2)}, u32[]{:S(2)}) %all-to-all-start.3) | async-done | bytes 5242912 | tf_op jit(solution)/shard_map/all_to_all | solution.py:112
  383.1 7.7 %copy.35 = bf16[40,32,2048]{2,1,0:T(8,128)(2,1)} copy(bf16[40,32,2048]{2,0,1:T(8,128)(2,1)} %bitcast.7) | data formatting | bytes 10485760 | tf_op jit(solution)/shard_map/reshape | solution.py:112
  390.8 9.1 %reshape_reshape.3 = bf16[40,128,512]{2,1,0:T(8,128)(2,1)} reshape(bf16[40,32,2048]{2,1,0:T(8,128)(2,1)} %copy.35) | data formatting | bytes 10485760 | tf_op jit(solution)/shard_map/reshape;reshape | solution.py:113
  (19 shorter events, 0.1 us)
Async XLA Ops:
  7.2 140.8 %reduce-scatter.2.cloned.1.call-start = ((), (), s32[]{:S(2)}) async-start(), calls=%async_computation.5 | async-start | bytes 5406720 | tf_op jit(solution)/shard_map/reduce_scatter | solution.py:89
  15.1 0.7 copy-start.4
  149.6 28.5 %copy-start.3 = (f32[1,2,128,512]{3,2,1,0:T(8,128)S(1)}, f32[1,2,128,512]{3,2,1,0:T(8,128)}, u32[]{:S(2)}) copy-start(f32[1,2,128,512]{3,2,1,0:T(8,128)} %param.5) | copy-start | bytes 1572868
  179.8 30.6 %all-to-all-start.1 = ((bf16[8,2,128,512]{3,2,1,0:T(8,128)(2,1)}), bf16[8,2,128,512]{3,2,1,0:T(8,128)(2,1)S(1)}, u32[]{:S(2)}, u32[]{:S(2)}) async-start(bf16[8,2,128,512]{3,2,1,0:T(8,128)(2,1)} %broadcast_in_dim.79), calls=%async_computation.2 | async-start | bytes 4194304 | tf_op jit(solution)/shard_map/all_to_all | solution.py:19
  215.7 3.1 copy-start
  221.0 3.1 copy-start.1
  226.3 3.1 copy-start.2
  237.1 20.8 %all-to-all-start.2 = ((bf16[2,32,2048]{2,0,1:T(2,128)(2,1)}), bf16[2,32,2048]{2,0,1:T(2,128)(2,1)S(1)}, u32[]{:S(2)}, u32[]{:S(2)}) async-start(bf16[2,32,2048]{2,0,1:T(2,128)(2,1)} %copy.33), calls=%async_computation.3 | async-start | bytes 524288 | tf_op jit(solution)/shard_map/all_to_all | solution.py:105
  261.8 121.3 %all-to-all-start.3 = ((bf16[32,40,2048]{2,1,0:T(8,128)(2,1)}), bf16[32,40,2048]{2,1,0:T(8,128)(2,1)}, u32[]{:S(2)}, u32[]{:S(2)}) async-start(bf16[32,40,2048]{2,1,0:T(8,128)(2,1)} %stack.2), calls=%async_computation.4 | async-start | bytes 10485760 | tf_op jit(solution)/shard_map/all_to_all | solution.py:112
Sparse Core Ops, SparseCore 0:
  15.3 132.6 reduce-scatter.1
